TPU v7x, 128 devices: a whole 4x4x4 slice. The times are simulated.
128 devices in a mesh: row: 8 (over x, y_lo), col: 8 (over z, core), band: 2 (over y_hi).
Axes of the slice: x: 4, y: 4 (y_hi: 2, y_lo: 2; y = y_hi * 2 + y_lo), z: 4, core: 2. Of those that a mesh axis runs over, the one named last changes fastest.
Arguments:
- freq_index: int32 [2], replicated, may hold values from 0 to 32
- band_energy: float32 [16], replicated, may hold values from -4 to 4
- pole_amp: float32 [8192, 8192], P('row', 'col'), may hold values from -6 to 6
- pole_freq: float32 [8192, 8192], P('row', 'col'), may hold values from 0.5 to 4
- left_pieces: bfloat16 [16, 256, 8192], P(('col', 'band'), None, 'row'), may hold values from -0.032958984 to 0.032958984
- right_pieces: bfloat16 [16, 256, 8192], P(('row', 'band'), None, 'col'), may hold values from -0.032958984 to 0.032958984
Outputs:
- sigma: float32 [2, 256, 256], P(None, ('row', 'col', 'band'))
All inputs are finite; a program needn't handle non-finite values.
Results may differ from a plain program's by a relative error of at most 0.0055.
Values may be sent and summed in bfloat16 or wider, within the bound.
A program may use at most 128 MiB of HBM per device.

v0:
```python
import jax
import jax.numpy as jnp
from jax import lax
from jax.sharding import Mesh
from jax.sharding import PartitionSpec as P

ROW = ("row_0", "row_1")
ROW_COL_BAND = ("row_0", "row_1", "col", "band")
ROW_BAND = ("row_0", "row_1", "band")


def whole_of(array, axes, dim):
    for axis in reversed(axes):
        array = lax.all_gather(array, axis, axis=dim, tiled=True)
    return array


def body(freq_index, band_energy, pole_amp, pole_freq, left_pieces, right_pieces):
    bpiece = left_pieces.shape[0]
    nstate = left_pieces.shape[1]
    nfreq = freq_index.shape[0]
    nband = lax.axis_size("band")
    group = lax.axis_index("band")
    freq = -4.0 + 0.25 * freq_index.astype(jnp.float32)
    right_all = whole_of(right_pieces, ROW, 0)

    def energy_at(position):
        overall = (position // bpiece * nband + group) * bpiece + position % bpiece
        return lax.dynamic_index_in_dim(band_energy, overall, 0, False)

    def add_band(total, left_band, position):
        right_band = lax.dynamic_index_in_dim(right_all, position, 0, False)
        energy = energy_at(position)
        results = []
        for w in range(nfreq):
            distance = freq[w] - energy - pole_freq
            screened = (pole_amp * distance / (distance * distance + 0.25)).astype(jnp.bfloat16)
            partial_value = jnp.dot(left_band, screened, preferred_element_type=jnp.float32).astype(
                jnp.bfloat16
            )
            results.append(
                lax.dot_general(
                    partial_value,
                    right_band,
                    (((1,), (1,)), ((), ())),
                    preferred_element_type=jnp.float32,
                )
            )
        return total + jnp.stack(results)

    start = jnp.zeros((nfreq, nstate, nstate), jnp.float32)
    left_all = lax.all_gather(left_pieces, "col", axis=0, tiled=True)

    def step(index, carry):
        left_band = lax.dynamic_index_in_dim(left_all, index, 0, False)
        return add_band(carry, left_band, index)

    total = lax.fori_loop(0, left_all.shape[0], step, start)
    summed = lax.psum(total, ROW_COL_BAND)
    owned = nstate // lax.axis_size(ROW_COL_BAND)
    sigma = lax.dynamic_slice_in_dim(summed, lax.axis_index(ROW_COL_BAND) * owned, owned, 1)
    return sigma


def solution(mesh):
    split = Mesh(
        mesh.devices.reshape(4, 2, mesh.shape["col"], mesh.shape["band"]),
        ("row_0", "row_1", "col", "band"),
    )
    in_specs = (
        P(),
        P(),
        P(ROW, "col"),
        P(ROW, "col"),
        P(("col", "band"), None, ROW),
        P(ROW_BAND, None, "col"),
    )
    out_specs = P(None, ROW_COL_BAND, None)
    return jax.shard_map(body, mesh=split, in_specs=in_specs, out_specs=out_specs, check_vma=False)
```

profile of v0, /device:TPU:1, one launch (start us, length us, event | category | flops | bytes accessed | tf_op | source)
XLA Modules:
  0.0 393.0 jit_solution(11050577234584993853)
XLA Ops:
  6.5 0.7 all-gather.6.cloned.1.call-update
  7.3 0.7 all-gather.4.cloned.1.call-update
  8.1 27.8 %all-gather.6.cloned.1.call-done = bf16[2,256,1024]{2,1,0:T(8,128)(2,1)} async-done(((bf16[1,256,1024]{2,1,0:T(8,128)(2,1)}), bf16[2,256,1024]{2,1,0:T(8,128)(2,1)}) %all-gather.6.cloned.1.call-update) | async-done | bytes 1048592 | tf_op jit(solution)/shard_map/all_gather | solution.py:14
  35.9 0.7 multiply_add_fusion
  36.6 34.8 %all-gather.4.cloned.1.call-done = bf16[8,256,1024]{2,1,0:T(8,128)(2,1)} async-done(((bf16[1,256,1024]{2,1,0:T(8,128)(2,1)}), bf16[8,256,1024]{2,1,0:T(8,128)(2,1)}) %all-gather.4.cloned.1.call-update) | async-done | bytes 4194320 | tf_op jit(solution)/shard_map/all_gather | solution.py:52
  71.4 49.1 %all-gather.8.cloned.1.call-done = bf16[8,256,1024]{2,1,0:T(8,128)(2,1)} async-done(((bf16[2,256,1024]{2,1,0:T(8,128)(2,1)}), bf16[8,256,1024]{2,1,0:T(8,128)(2,1)}) %all-gather.8.cloned.1.call-update) | async-done | bytes 4194320 | tf_op jit(solution)/shard_map/all_gather | solution.py:14
  120.5 116.6 %while.17 = (s32[]{:T(128)}, f32[2,256,256]{2,1,0:T(8,128)S(1)}, bf16[8,256,1024]{2,1,0:T(8,128)(2,1)}, f32[2]{0:T(128)S(1)}, s32[]{:T(128)}, /*index=5*/f32[16]...) while((s32[]{:T(128)}, f32[2,256,256]{2,1,0:T(8,128)S(1)}, ...), condition=%wide.region_1.2_spmd.clone, body=%wide.region_0.1_spmd.clone.sunk | while | flops 1355677696 | bytes 20974844 | solution.py:58
  120.5 1.2 dynamic_slice.70
  121.7 0.6 fusion.34
  124.7 5.1 %convolution_bitcast_fusion.4 = f32[1,256,256]{2,1,0:T(8,128)S(1)} fusion(f32[1024,1024]{1,0:T(8,128)} %get-tuple-element.398, f32[1024,1024]{1,0:T(8,128)} %get-tuple-element.397, f32[]{:T(128)} %bitcast.32, bf16[8,256,1024]{2,1,0:T(8,128)(2,1)} %get-tuple-element.399, s32[]{:T(128)S(6)} %copy.9, bf16[8,256,1024]{2,1,0:T(8,128)(2,1)} %get-tuple-element.393), kind=kOutput, calls=%fused_computation.6.clone.1 | convolution fusion | flops 677642240 | bytes 9700864 | tf_op jit(solution)/shard_map/while/body/eval_jaxpr/dot_general | solution.py:42
  129.8 5.1 %convolution_bitcast_fusion.5 = f32[1,256,256]{2,1,0:T(8,128)S(1)} fusion(f32[1024,1024]{1,0:T(8,128)} %get-tuple-element.398, f32[1024,1024]{1,0:T(8,128)} %get-tuple-element.397, f32[]{:T(128)} %bitcast.33, bf16[8,256,1024]{2,1,0:T(8,128)(2,1)} %get-tuple-element.399, s32[]{:T(128)S(6)} %copy.9, bf16[8,256,1024]{2,1,0:T(8,128)(2,1)} %get-tuple-element.393), kind=kOutput, calls=%fused_computation.7.clone.1 | convolution fusion | flops 677642240 | bytes 9700864 | tf_op jit(solution)/shard_map/while/body/eval_jaxpr/dot_general | solution.py:42
  134.9 0.1 maximum_add_fusion.2
  135.1 1.2 dynamic_slice.70
  136.3 0.6 fusion.34
  139.3 5.1 %convolution_bitcast_fusion.4 = f32[1,256,256]{2,1,0:T(8,128)S(1)} fusion(f32[1024,1024]{1,0:T(8,128)} %get-tuple-element.398, f32[1024,1024]{1,0:T(8,128)} %get-tuple-element.397, f32[]{:T(128)} %bitcast.32, bf16[8,256,1024]{2,1,0:T(8,128)(2,1)} %get-tuple-element.399, s32[]{:T(128)S(6)} %copy.9, bf16[8,256,1024]{2,1,0:T(8,128)(2,1)} %get-tuple-element.393), kind=kOutput, calls=%fused_computation.6.clone.1 | convolution fusion | flops 677642240 | bytes 9700864 | tf_op jit(solution)/shard_map/while/body/eval_jaxpr/dot_general | solution.py:42
  144.4 5.1 %convolution_bitcast_fusion.5 = f32[1,256,256]{2,1,0:T(8,128)S(1)} fusion(f32[1024,1024]{1,0:T(8,128)} %get-tuple-element.398, f32[1024,1024]{1,0:T(8,128)} %get-tuple-element.397, f32[]{:T(128)} %bitcast.33, bf16[8,256,1024]{2,1,0:T(8,128)(2,1)} %get-tuple-element.399, s32[]{:T(128)S(6)} %copy.9, bf16[8,256,1024]{2,1,0:T(8,128)(2,1)} %get-tuple-element.393), kind=kOutput, calls=%fused_computation.7.clone.1 | convolution fusion | flops 677642240 | bytes 9700864 | tf_op jit(solution)/shard_map/while/body/eval_jaxpr/dot_general | solution.py:42
  149.4 0.1 maximum_add_fusion.2
  149.6 1.2 dynamic_slice.70
  150.9 0.6 fusion.34
  153.9 5.1 %convolution_bitcast_fusion.4 = f32[1,256,256]{2,1,0:T(8,128)S(1)} fusion(f32[1024,1024]{1,0:T(8,128)} %get-tuple-element.398, f32[1024,1024]{1,0:T(8,128)} %get-tuple-element.397, f32[]{:T(128)} %bitcast.32, bf16[8,256,1024]{2,1,0:T(8,128)(2,1)} %get-tuple-element.399, s32[]{:T(128)S(6)} %copy.9, bf16[8,256,1024]{2,1,0:T(8,128)(2,1)} %get-tuple-element.393), kind=kOutput, calls=%fused_computation.6.clone.1 | convolution fusion | flops 677642240 | bytes 9700864 | tf_op jit(solution)/shard_map/while/body/eval_jaxpr/dot_general | solution.py:42
  159.0 5.1 %convolution_bitcast_fusion.5 = f32[1,256,256]{2,1,0:T(8,128)S(1)} fusion(f32[1024,1024]{1,0:T(8,128)} %get-tuple-element.398, f32[1024,1024]{1,0:T(8,128)} %get-tuple-element.397, f32[]{:T(128)} %bitcast.33, bf16[8,256,1024]{2,1,0:T(8,128)(2,1)} %get-tuple-element.399, s32[]{:T(128)S(6)} %copy.9, bf16[8,256,1024]{2,1,0:T(8,128)(2,1)} %get-tuple-element.393), kind=kOutput, calls=%fused_computation.7.clone.1 | convolution fusion | flops 677642240 | bytes 9700864 | tf_op jit(solution)/shard_map/while/body/eval_jaxpr/dot_general | solution.py:42
  164.0 0.1 maximum_add_fusion.2
  164.2 1.2 dynamic_slice.70
  165.5 0.6 fusion.34
  168.5 5.1 %convolution_bitcast_fusion.4 = f32[1,256,256]{2,1,0:T(8,128)S(1)} fusion(f32[1024,1024]{1,0:T(8,128)} %get-tuple-element.398, f32[1024,1024]{1,0:T(8,128)} %get-tuple-element.397, f32[]{:T(128)} %bitcast.32, bf16[8,256,1024]{2,1,0:T(8,128)(2,1)} %get-tuple-element.399, s32[]{:T(128)S(6)} %copy.9, bf16[8,256,1024]{2,1,0:T(8,128)(2,1)} %get-tuple-element.393), kind=kOutput, calls=%fused_computation.6.clone.1 | convolution fusion | flops 677642240 | bytes 9700864 | tf_op jit(solution)/shard_map/while/body/eval_jaxpr/dot_general | solution.py:42
  173.5 5.1 %convolution_bitcast_fusion.5 = f32[1,256,256]{2,1,0:T(8,128)S(1)} fusion(f32[1024,1024]{1,0:T(8,128)} %get-tuple-element.398, f32[1024,1024]{1,0:T(8,128)} %get-tuple-element.397, f32[]{:T(128)} %bitcast.33, bf16[8,256,1024]{2,1,0:T(8,128)(2,1)} %get-tuple-element.399, s32[]{:T(128)S(6)} %copy.9, bf16[8,256,1024]{2,1,0:T(8,128)(2,1)} %get-tuple-element.393), kind=kOutput, calls=%fused_computation.7.clone.1 | convolution fusion | flops 677642240 | bytes 9700864 | tf_op jit(solution)/shard_map/while/body/eval_jaxpr/dot_general | solution.py:42
  178.6 0.1 maximum_add_fusion.2
  178.8 1.2 dynamic_slice.70
  180.0 0.6 fusion.34
  183.0 5.1 %convolution_bitcast_fusion.4 = f32[1,256,256]{2,1,0:T(8,128)S(1)} fusion(f32[1024,1024]{1,0:T(8,128)} %get-tuple-element.398, f32[1024,1024]{1,0:T(8,128)} %get-tuple-element.397, f32[]{:T(128)} %bitcast.32, bf16[8,256,1024]{2,1,0:T(8,128)(2,1)} %get-tuple-element.399, s32[]{:T(128)S(6)} %copy.9, bf16[8,256,1024]{2,1,0:T(8,128)(2,1)} %get-tuple-element.393), kind=kOutput, calls=%fused_computation.6.clone.1 | convolution fusion | flops 677642240 | bytes 9700864 | tf_op jit(solution)/shard_map/while/body/eval_jaxpr/dot_general | solution.py:42
  188.1 5.1 %convolution_bitcast_fusion.5 = f32[1,256,256]{2,1,0:T(8,128)S(1)} fusion(f32[1024,1024]{1,0:T(8,128)} %get-tuple-element.398, f32[1024,1024]{1,0:T(8,128)} %get-tuple-element.397, f32[]{:T(128)} %bitcast.33, bf16[8,256,1024]{2,1,0:T(8,128)(2,1)} %get-tuple-element.399, s32[]{:T(128)S(6)} %copy.9, bf16[8,256,1024]{2,1,0:T(8,128)(2,1)} %get-tuple-element.393), kind=kOutput, calls=%fused_computation.7.clone.1 | convolution fusion | flops 677642240 | bytes 9700864 | tf_op jit(solution)/shard_map/while/body/eval_jaxpr/dot_general | solution.py:42
  193.2 0.1 maximum_add_fusion.2
  193.4 1.2 dynamic_slice.70
  194.6 0.6 fusion.34
  197.6 5.1 %convolution_bitcast_fusion.4 = f32[1,256,256]{2,1,0:T(8,128)S(1)} fusion(f32[1024,1024]{1,0:T(8,128)} %get-tuple-element.398, f32[1024,1024]{1,0:T(8,128)} %get-tuple-element.397, f32[]{:T(128)} %bitcast.32, bf16[8,256,1024]{2,1,0:T(8,128)(2,1)} %get-tuple-element.399, s32[]{:T(128)S(6)} %copy.9, bf16[8,256,1024]{2,1,0:T(8,128)(2,1)} %get-tuple-element.393), kind=kOutput, calls=%fused_computation.6.clone.1 | convolution fusion | flops 677642240 | bytes 9700864 | tf_op jit(solution)/shard_map/while/body/eval_jaxpr/dot_general | solution.py:42
  202.7 5.1 %convolution_bitcast_fusion.5 = f32[1,256,256]{2,1,0:T(8,128)S(1)} fusion(f32[1024,1024]{1,0:T(8,128)} %get-tuple-element.398, f32[1024,1024]{1,0:T(8,128)} %get-tuple-element.397, f32[]{:T(128)} %bitcast.33, bf16[8,256,1024]{2,1,0:T(8,128)(2,1)} %get-tuple-element.399, s32[]{:T(128)S(6)} %copy.9, bf16[8,256,1024]{2,1,0:T(8,128)(2,1)} %get-tuple-element.393), kind=kOutput, calls=%fused_computation.7.clone.1 | convolution fusion | flops 677642240 | bytes 9700864 | tf_op jit(solution)/shard_map/while/body/eval_jaxpr/dot_general | solution.py:42
  207.8 0.1 maximum_add_fusion.2
  208.0 1.2 dynamic_slice.70
  209.2 0.6 fusion.34
  212.2 5.1 %convolution_bitcast_fusion.4 = f32[1,256,256]{2,1,0:T(8,128)S(1)} fusion(f32[1024,1024]{1,0:T(8,128)} %get-tuple-element.398, f32[1024,1024]{1,0:T(8,128)} %get-tuple-element.397, f32[]{:T(128)} %bitcast.32, bf16[8,256,1024]{2,1,0:T(8,128)(2,1)} %get-tuple-element.399, s32[]{:T(128)S(6)} %copy.9, bf16[8,256,1024]{2,1,0:T(8,128)(2,1)} %get-tuple-element.393), kind=kOutput, calls=%fused_computation.6.clone.1 | convolution fusion | flops 677642240 | bytes 9700864 | tf_op jit(solution)/shard_map/while/body/eval_jaxpr/dot_general | solution.py:42
  217.3 5.1 %convolution_bitcast_fusion.5 = f32[1,256,256]{2,1,0:T(8,128)S(1)} fusion(f32[1024,1024]{1,0:T(8,128)} %get-tuple-element.398, f32[1024,1024]{1,0:T(8,128)} %get-tuple-element.397, f32[]{:T(128)} %bitcast.33, bf16[8,256,1024]{2,1,0:T(8,128)(2,1)} %get-tuple-element.399, s32[]{:T(128)S(6)} %copy.9, bf16[8,256,1024]{2,1,0:T(8,128)(2,1)} %get-tuple-element.393), kind=kOutput, calls=%fused_computation.7.clone.1 | convolution fusion | flops 677642240 | bytes 9700864 | tf_op jit(solution)/shard_map/while/body/eval_jaxpr/dot_general | solution.py:42
  222.5 1.2 dynamic_slice.70
  223.8 0.6 fusion.34
  226.8 5.1 %convolution_bitcast_fusion.4 = f32[1,256,256]{2,1,0:T(8,128)S(1)} fusion(f32[1024,1024]{1,0:T(8,128)} %get-tuple-element.398, f32[1024,1024]{1,0:T(8,128)} %get-tuple-element.397, f32[]{:T(128)} %bitcast.32, bf16[8,256,1024]{2,1,0:T(8,128)(2,1)} %get-tuple-element.399, s32[]{:T(128)S(6)} %copy.9, bf16[8,256,1024]{2,1,0:T(8,128)(2,1)} %get-tuple-element.393), kind=kOutput, calls=%fused_computation.6.clone.1 | convolution fusion | flops 677642240 | bytes 9700864 | tf_op jit(solution)/shard_map/while/body/eval_jaxpr/dot_general | solution.py:42
  231.9 5.1 %convolution_bitcast_fusion.5 = f32[1,256,256]{2,1,0:T(8,128)S(1)} fusion(f32[1024,1024]{1,0:T(8,128)} %get-tuple-element.398, f32[1024,1024]{1,0:T(8,128)} %get-tuple-element.397, f32[]{:T(128)} %bitcast.33, bf16[8,256,1024]{2,1,0:T(8,128)(2,1)} %get-tuple-element.399, s32[]{:T(128)S(6)} %copy.9, bf16[8,256,1024]{2,1,0:T(8,128)(2,1)} %get-tuple-element.393), kind=kOutput, calls=%fused_computation.7.clone.1 | convolution fusion | flops 677642240 | bytes 9700864 | tf_op jit(solution)/shard_map/while/body/eval_jaxpr/dot_general | solution.py:42
  237.1 0.8 copy-done
  237.9 147.2 %all-reduce.2.cloned.1.call-done = f32[2,256,256]{2,1,0:T(8,128)} async-done(((f32[2,256,256]{2,1,0:T(8,128)}), f32[2,256,256]{2,1,0:T(8,128)}) %all-reduce.2.cloned.1.call-update) | async-done | bytes 524304 | tf_op jit(solution)/shard_map/psum | solution.py:59
  385.1 1.3 constant_dynamic-slice_fusion
  (10 shorter events, 0.4 us)
Async XLA Ops:
  6.5 29.3 %all-gather.6.cloned.1.call-start = ((), (), s32[]{:S(2)}) async-start(), calls=%async_computation.1 | async-start | bytes 1572864 | tf_op jit(solution)/shard_map/all_gather | solution.py:14
  7.3 64.2 %all-gather.4.cloned.1.call-start = ((), (), s32[]{:S(2)}) async-start(), calls=%async_computation | async-start | bytes 4718592 | tf_op jit(solution)/shard_map/all_gather | solution.py:52
  8.0 112.5 %all-gather.8.cloned.1.call-start = ((), (), s32[]{:S(2)}) async-start(), calls=%async_computation.2 | async-start | bytes 5242880 | tf_op jit(solution)/shard_map/all_gather | solution.py:14
  35.9 349.2 %all-reduce.2.cloned.1.call-start = ((), (), s32[]{:S(2)}) async-start(), calls=%async_computation.3 | async-start | bytes 1048576 | tf_op jit(solution)/shard_map/psum | solution.py:59
  237.1 0.8 copy-start
Sparse Core Ops, SparseCore 0:
  9.0 26.8 all-gather.5
  37.6 33.7 all-gather.3
  73.1 47.3 all-gather.7
  238.0 147.0 all-reduce.1
where the time goes:
time: 393 us
  waiting for transfers between devices  260 us (66%)
  matrix products  81.2 us (21%)
  loops' own time  19.2 us (5%)
  local copies, waits for them, and re-layouts  17.1 us (4%)
  between operations  13.2 us (3%)
    psum x1, waiting for transfers between devices, body(): summed = lax.psum(total, ROW_COL_BAND)  147 us
    dot_general x16, matrix products, add_band(): lax.dot_general(partial_value, right_band, (((1,), (1,)), ((), ())), pref...  81.2 us
    all_gather x2, waiting for transfers between devices, whole_of(): array = lax.all_gather(array, axis, axis=dim, tiled=True)  76.9 us
    all_gather x1, waiting for transfers between devices, body(): left_all = lax.all_gather(left_pieces, 'col', axis=0, tiled=True)  34.8 us
    another operation x1, loops' own time, body(): total = lax.fori_loop(0, left_all.shape[0], step, start)  19.2 us
    dynamic_slice x8, local copies, waits for them, and re-layouts, energy_at(): return lax.dynamic_index_in_dim(band_energy, overall, 0, False)  9.87 us
  transfers between devices with their start and end apart: 4, of which 4 were waited for; matrix products, arithmetic and copies ran while one was open for 0% of the time, Pallas kernels for 0%

commit v1 on v0

--- a/solution.py
+++ b/solution.py
@@ -49,7 +49,9 @@
         return total + jnp.stack(results)
 
     start = jnp.zeros((nfreq, nstate, nstate), jnp.float32)
-    left_all = lax.all_gather(left_pieces, "col", axis=0, tiled=True)
+    left_all = jnp.concatenate(
+        lax.all_to_all(jnp.stack([left_pieces] * lax.axis_size("col")), "col", 0, 0), axis=0
+    )
 
     def step(index, carry):
         left_band = lax.dynamic_index_in_dim(left_all, index, 0, False)

time: 393 us -> 360 us (0.916)
  waiting for transfers between devices: 260 us -> 224 us
  starting transfers between devices: 0.12 us -> 5.44 us
    all_to_all x0 -> x1, waiting for transfers between devices: none -> 48.8 us  [body(): lax.all_to_all(jnp.stack([left_pieces] * lax.axis_size('col')), 'col', 0, 0)]
    all_gather x2, waiting for transfers between devices: 76.9 us -> 28.6 us  [whole_of(): array = lax.all_gather(array, axis, axis=dim, tiled=True)]
    all_gather x1 -> x0, waiting for transfers between devices: 34.8 us -> none  [body(): left_all = lax.all_gather(left_pieces, 'col', axis=0, tiled=True)]
    all_to_all x0 -> x1, starting transfers between devices: none -> 5.39 us  [body(): lax.all_to_all(jnp.stack([left_pieces] * lax.axis_size('col')), 'col', 0, 0)]
    dynamic_slice x8, local copies, waits for them, and re-layouts: 9.87 us -> 4.63 us  [energy_at(): return lax.dynamic_index_in_dim(band_energy, overall, 0, False)]
  transfers between devices with their start and end apart: 4 -> 4, of which waited for: 4 -> 3; matrix products, arithmetic and copies ran while one was open for 0% -> 1% of each run, Pallas kernels for 0% -> 0%
where the time goes in v1:
time: 360 us
  waiting for transfers between devices  224 us (62%)
  matrix products  81 us (22%)
  loops' own time  19.3 us (5%)
  local copies, waits for them, and re-layouts  15.4 us (4%)
  between operations  13.1 us (4%)
  starting transfers between devices  5.44 us (2%)
    psum x1, waiting for transfers between devices, body(): summed = lax.psum(total, ROW_COL_BAND)  146 us
    dot_general x16, matrix products, add_band(): lax.dot_general(partial_value, right_band, (((1,), (1,)), ((), ())), pref...  81 us
    all_to_all x1, waiting for transfers between devices, body(): lax.all_to_all(jnp.stack([left_pieces] * lax.axis_size('col')), 'col', 0, 0)  48.8 us
    all_gather x2, waiting for transfers between devices, whole_of(): array = lax.all_gather(array, axis, axis=dim, tiled=True)  28.6 us
    another operation x1, loops' own time, body(): total = lax.fori_loop(0, left_all.shape[0], step, start)  19.3 us
  transfers between devices with their start and end apart: 4, of which 3 were waited for; matrix products, arithmetic and copies ran while one was open for 1% of the time, Pallas kernels for 0%

profile of v1, /device:TPU:1, one launch (start us, length us, event | category | flops | bytes accessed | tf_op | source)
XLA Modules:
  0.0 359.6 jit_solution(10050549751825338046)
XLA Ops:
  6.5 0.7 all-gather.3.cloned.1.call-update
  7.3 28.6 %all-gather.3.cloned.1.call-done = bf16[2,256,1024]{2,1,0:T(8,128)(2,1)} async-done(((bf16[1,256,1024]{2,1,0:T(8,128)(2,1)}), bf16[2,256,1024]{2,1,0:T(8,128)(2,1)}) %all-gather.3.cloned.1.call-update) | async-done | bytes 1048592 | tf_op jit(solution)/shard_map/all_gather | solution.py:14
  35.9 3.5 stack.44
  39.4 5.4 %all-to-all-start = ((bf16[8,1,256,1024]{3,2,1,0:T(8,128)(2,1)}), bf16[8,1,256,1024]{3,2,1,0:T(8,128)(2,1)}, u32[]{:S(2)}, u32[]{:S(2)}) async-start(bf16[8,1,256,1024]{3,2,1,0:T(8,128)(2,1)} %stack.44), calls=%async_computation | async-start | bytes 8388608 | tf_op jit(solution)/shard_map/all_to_all | solution.py:53
  44.9 48.8 %all-to-all-done = bf16[8,1,256,1024]{3,2,1,0:T(8,128)(2,1)} async-done(((bf16[8,1,256,1024]{3,2,1,0:T(8,128)(2,1)}), bf16[8,1,256,1024]{3,2,1,0:T(8,128)(2,1)}, u32[]{:S(2)}, u32[]{:S(2)}) %all-to-all-start) | async-done | bytes 4194336 | tf_op jit(solution)/shard_map/all_to_all | solution.py:53
  93.6 111.3 %while.17 = (s32[]{:T(128)}, f32[2,256,256]{2,1,0:T(8,128)S(1)}, bf16[8,256,1024]{2,1,0:T(8,128)(2,1)}, f32[2]{0:T(128)S(1)}, s32[]{:T(128)}, /*index=5*/f32[16]...) while((s32[]{:T(128)}, f32[2,256,256]{2,1,0:T(8,128)S(1)}, ...), condition=%wide.region_1.2_spmd.clone, body=%wide.region_0.1_spmd.clone.sunk | while | flops 1355677696 | bytes 20974836 | solution.py:60
  93.6 0.6 dynamic_slice.70
  94.2 0.6 fusion.34
  96.0 5.1 %convolution_bitcast_fusion.5 = f32[1,256,256]{2,1,0:T(8,128)S(1)} fusion(f32[1024,1024]{1,0:T(8,128)} %get-tuple-element.398, f32[1024,1024]{1,0:T(8,128)} %get-tuple-element.397, f32[]{:T(128)} %bitcast.35, bf16[8,256,1024]{2,1,0:T(8,128)(2,1)} %get-tuple-element.399, s32[]{:T(128)} %get-tuple-element.378, bf16[8,256,1024]{2,1,0:T(8,128)(2,1)} %get-tuple-element.393), kind=kOutput, calls=%fused_computation.7.clone.1 | convolution fusion | flops 677642240 | bytes 9700864 | tf_op jit(solution)/shard_map/while/body/eval_jaxpr/dot_general | solution.py:42
  102.3 5.1 %convolution_bitcast_fusion.4 = f32[1,256,256]{2,1,0:T(8,128)S(1)} fusion(f32[1024,1024]{1,0:T(8,128)} %get-tuple-element.398, f32[1024,1024]{1,0:T(8,128)} %get-tuple-element.397, f32[]{:T(128)} %bitcast.34, bf16[8,256,1024]{2,1,0:T(8,128)(2,1)} %get-tuple-element.399, s32[]{:T(128)} %get-tuple-element.378, bf16[8,256,1024]{2,1,0:T(8,128)(2,1)} %get-tuple-element.393), kind=kOutput, calls=%fused_computation.6.clone.1 | convolution fusion | flops 677642240 | bytes 9700864 | tf_op jit(solution)/shard_map/while/body/eval_jaxpr/dot_general | solution.py:42
  107.4 0.1 maximum_add_fusion.2
  107.5 0.6 dynamic_slice.70
  108.1 0.6 fusion.34
  110.0 5.1 %convolution_bitcast_fusion.5 = f32[1,256,256]{2,1,0:T(8,128)S(1)} fusion(f32[1024,1024]{1,0:T(8,128)} %get-tuple-element.398, f32[1024,1024]{1,0:T(8,128)} %get-tuple-element.397, f32[]{:T(128)} %bitcast.35, bf16[8,256,1024]{2,1,0:T(8,128)(2,1)} %get-tuple-element.399, s32[]{:T(128)} %get-tuple-element.378, bf16[8,256,1024]{2,1,0:T(8,128)(2,1)} %get-tuple-element.393), kind=kOutput, calls=%fused_computation.7.clone.1 | convolution fusion | flops 677642240 | bytes 9700864 | tf_op jit(solution)/shard_map/while/body/eval_jaxpr/dot_general | solution.py:42
  116.2 5.1 %convolution_bitcast_fusion.4 = f32[1,256,256]{2,1,0:T(8,128)S(1)} fusion(f32[1024,1024]{1,0:T(8,128)} %get-tuple-element.398, f32[1024,1024]{1,0:T(8,128)} %get-tuple-element.397, f32[]{:T(128)} %bitcast.34, bf16[8,256,1024]{2,1,0:T(8,128)(2,1)} %get-tuple-element.399, s32[]{:T(128)} %get-tuple-element.378, bf16[8,256,1024]{2,1,0:T(8,128)(2,1)} %get-tuple-element.393), kind=kOutput, calls=%fused_computation.6.clone.1 | convolution fusion | flops 677642240 | bytes 9700864 | tf_op jit(solution)/shard_map/while/body/eval_jaxpr/dot_general | solution.py:42
  121.3 0.1 maximum_add_fusion.2
  121.5 0.6 dynamic_slice.70
  122.0 0.6 fusion.34
  123.9 5.1 %convolution_bitcast_fusion.5 = f32[1,256,256]{2,1,0:T(8,128)S(1)} fusion(f32[1024,1024]{1,0:T(8,128)} %get-tuple-element.398, f32[1024,1024]{1,0:T(8,128)} %get-tuple-element.397, f32[]{:T(128)} %bitcast.35, bf16[8,256,1024]{2,1,0:T(8,128)(2,1)} %get-tuple-element.399, s32[]{:T(128)} %get-tuple-element.378, bf16[8,256,1024]{2,1,0:T(8,128)(2,1)} %get-tuple-element.393), kind=kOutput, calls=%fused_computation.7.clone.1 | convolution fusion | flops 677642240 | bytes 9700864 | tf_op jit(solution)/shard_map/while/body/eval_jaxpr/dot_general | solution.py:42
  130.1 5.1 %convolution_bitcast_fusion.4 = f32[1,256,256]{2,1,0:T(8,128)S(1)} fusion(f32[1024,1024]{1,0:T(8,128)} %get-tuple-element.398, f32[1024,1024]{1,0:T(8,128)} %get-tuple-element.397, f32[]{:T(128)} %bitcast.34, bf16[8,256,1024]{2,1,0:T(8,128)(2,1)} %get-tuple-element.399, s32[]{:T(128)} %get-tuple-element.378, bf16[8,256,1024]{2,1,0:T(8,128)(2,1)} %get-tuple-element.393), kind=kOutput, calls=%fused_computation.6.clone.1 | convolution fusion | flops 677642240 | bytes 9700864 | tf_op jit(solution)/shard_map/while/body/eval_jaxpr/dot_general | solution.py:42
  135.2 0.1 maximum_add_fusion.2
  135.4 0.6 dynamic_slice.70
  136.0 0.6 fusion.34
  137.8 5.1 %convolution_bitcast_fusion.5 = f32[1,256,256]{2,1,0:T(8,128)S(1)} fusion(f32[1024,1024]{1,0:T(8,128)} %get-tuple-element.398, f32[1024,1024]{1,0:T(8,128)} %get-tuple-element.397, f32[]{:T(128)} %bitcast.35, bf16[8,256,1024]{2,1,0:T(8,128)(2,1)} %get-tuple-element.399, s32[]{:T(128)} %get-tuple-element.378, bf16[8,256,1024]{2,1,0:T(8,128)(2,1)} %get-tuple-element.393), kind=kOutput, calls=%fused_computation.7.clone.1 | convolution fusion | flops 677642240 | bytes 9700864 | tf_op jit(solution)/shard_map/while/body/eval_jaxpr/dot_general | solution.py:42
  144.0 5.1 %convolution_bitcast_fusion.4 = f32[1,256,256]{2,1,0:T(8,128)S(1)} fusion(f32[1024,1024]{1,0:T(8,128)} %get-tuple-element.398, f32[1024,1024]{1,0:T(8,128)} %get-tuple-element.397, f32[]{:T(128)} %bitcast.34, bf16[8,256,1024]{2,1,0:T(8,128)(2,1)} %get-tuple-element.399, s32[]{:T(128)} %get-tuple-element.378, bf16[8,256,1024]{2,1,0:T(8,128)(2,1)} %get-tuple-element.393), kind=kOutput, calls=%fused_computation.6.clone.1 | convolution fusion | flops 677642240 | bytes 9700864 | tf_op jit(solution)/shard_map/while/body/eval_jaxpr/dot_general | solution.py:42
  149.1 0.1 maximum_add_fusion.2
  149.3 0.6 dynamic_slice.70
  149.9 0.6 fusion.34
  151.7 5.1 %convolution_bitcast_fusion.5 = f32[1,256,256]{2,1,0:T(8,128)S(1)} fusion(f32[1024,1024]{1,0:T(8,128)} %get-tuple-element.398, f32[1024,1024]{1,0:T(8,128)} %get-tuple-element.397, f32[]{:T(128)} %bitcast.35, bf16[8,256,1024]{2,1,0:T(8,128)(2,1)} %get-tuple-element.399, s32[]{:T(128)} %get-tuple-element.378, bf16[8,256,1024]{2,1,0:T(8,128)(2,1)} %get-tuple-element.393), kind=kOutput, calls=%fused_computation.7.clone.1 | convolution fusion | flops 677642240 | bytes 9700864 | tf_op jit(solution)/shard_map/while/body/eval_jaxpr/dot_general | solution.py:42
  157.9 5.1 %convolution_bitcast_fusion.4 = f32[1,256,256]{2,1,0:T(8,128)S(1)} fusion(f32[1024,1024]{1,0:T(8,128)} %get-tuple-element.398, f32[1024,1024]{1,0:T(8,128)} %get-tuple-element.397, f32[]{:T(128)} %bitcast.34, bf16[8,256,1024]{2,1,0:T(8,128)(2,1)} %get-tuple-element.399, s32[]{:T(128)} %get-tuple-element.378, bf16[8,256,1024]{2,1,0:T(8,128)(2,1)} %get-tuple-element.393), kind=kOutput, calls=%fused_computation.6.clone.1 | convolution fusion | flops 677642240 | bytes 9700864 | tf_op jit(solution)/shard_map/while/body/eval_jaxpr/dot_general | solution.py:42
  163.0 0.1 maximum_add_fusion.2
  163.2 0.6 dynamic_slice.70
  163.8 0.6 fusion.34
  165.6 5.1 %convolution_bitcast_fusion.5 = f32[1,256,256]{2,1,0:T(8,128)S(1)} fusion(f32[1024,1024]{1,0:T(8,128)} %get-tuple-element.398, f32[1024,1024]{1,0:T(8,128)} %get-tuple-element.397, f32[]{:T(128)} %bitcast.35, bf16[8,256,1024]{2,1,0:T(8,128)(2,1)} %get-tuple-element.399, s32[]{:T(128)} %get-tuple-element.378, bf16[8,256,1024]{2,1,0:T(8,128)(2,1)} %get-tuple-element.393), kind=kOutput, calls=%fused_computation.7.clone.1 | convolution fusion | flops 677642240 | bytes 9700864 | tf_op jit(solution)/shard_map/while/body/eval_jaxpr/dot_general | solution.py:42
  171.9 5.1 %convolution_bitcast_fusion.4 = f32[1,256,256]{2,1,0:T(8,128)S(1)} fusion(f32[1024,1024]{1,0:T(8,128)} %get-tuple-element.398, f32[1024,1024]{1,0:T(8,128)} %get-tuple-element.397, f32[]{:T(128)} %bitcast.34, bf16[8,256,1024]{2,1,0:T(8,128)(2,1)} %get-tuple-element.399, s32[]{:T(128)} %get-tuple-element.378, bf16[8,256,1024]{2,1,0:T(8,128)(2,1)} %get-tuple-element.393), kind=kOutput, calls=%fused_computation.6.clone.1 | convolution fusion | flops 677642240 | bytes 9700864 | tf_op jit(solution)/shard_map/while/body/eval_jaxpr/dot_general | solution.py:42
  176.9 0.1 maximum_add_fusion.2
  177.1 0.6 dynamic_slice.70
  177.7 0.6 fusion.34
  179.5 5.1 %convolution_bitcast_fusion.5 = f32[1,256,256]{2,1,0:T(8,128)S(1)} fusion(f32[1024,1024]{1,0:T(8,128)} %get-tuple-element.398, f32[1024,1024]{1,0:T(8,128)} %get-tuple-element.397, f32[]{:T(128)} %bitcast.35, bf16[8,256,1024]{2,1,0:T(8,128)(2,1)} %get-tuple-element.399, s32[]{:T(128)} %get-tuple-element.378, bf16[8,256,1024]{2,1,0:T(8,128)(2,1)} %get-tuple-element.393), kind=kOutput, calls=%fused_computation.7.clone.1 | convolution fusion | flops 677642240 | bytes 9700864 | tf_op jit(solution)/shard_map/while/body/eval_jaxpr/dot_general | solution.py:42
  185.8 5.1 %convolution_bitcast_fusion.4 = f32[1,256,256]{2,1,0:T(8,128)S(1)} fusion(f32[1024,1024]{1,0:T(8,128)} %get-tuple-element.398, f32[1024,1024]{1,0:T(8,128)} %get-tuple-element.397, f32[]{:T(128)} %bitcast.34, bf16[8,256,1024]{2,1,0:T(8,128)(2,1)} %get-tuple-element.399, s32[]{:T(128)} %get-tuple-element.378, bf16[8,256,1024]{2,1,0:T(8,128)(2,1)} %get-tuple-element.393), kind=kOutput, calls=%fused_computation.6.clone.1 | convolution fusion | flops 677642240 | bytes 9700864 | tf_op jit(solution)/shard_map/while/body/eval_jaxpr/dot_general | solution.py:42
  190.8 0.1 maximum_add_fusion.2
  191.0 0.6 dynamic_slice.70
  191.6 0.6 fusion.34
  193.4 5.1 %convolution_bitcast_fusion.5 = f32[1,256,256]{2,1,0:T(8,128)S(1)} fusion(f32[1024,1024]{1,0:T(8,128)} %get-tuple-element.398, f32[1024,1024]{1,0:T(8,128)} %get-tuple-element.397, f32[]{:T(128)} %bitcast.35, bf16[8,256,1024]{2,1,0:T(8,128)(2,1)} %get-tuple-element.399, s32[]{:T(128)} %get-tuple-element.378, bf16[8,256,1024]{2,1,0:T(8,128)(2,1)} %get-tuple-element.393), kind=kOutput, calls=%fused_computation.7.clone.1 | convolution fusion | flops 677642240 | bytes 9700864 | tf_op jit(solution)/shard_map/while/body/eval_jaxpr/dot_general | solution.py:42
  199.7 5.1 %convolution_bitcast_fusion.4 = f32[1,256,256]{2,1,0:T(8,128)S(1)} fusion(f32[1024,1024]{1,0:T(8,128)} %get-tuple-element.398, f32[1024,1024]{1,0:T(8,128)} %get-tuple-element.397, f32[]{:T(128)} %bitcast.34, bf16[8,256,1024]{2,1,0:T(8,128)(2,1)} %get-tuple-element.399, s32[]{:T(128)} %get-tuple-element.378, bf16[8,256,1024]{2,1,0:T(8,128)(2,1)} %get-tuple-element.393), kind=kOutput, calls=%fused_computation.6.clone.1 | convolution fusion | flops 677642240 | bytes 9700864 | tf_op jit(solution)/shard_map/while/body/eval_jaxpr/dot_general | solution.py:42
  204.9 0.8 copy-done
  205.7 146.0 %all-reduce.2.cloned.1.call-done = f32[2,256,256]{2,1,0:T(8,128)} async-done(((f32[2,256,256]{2,1,0:T(8,128)}), f32[2,256,256]{2,1,0:T(8,128)}) %all-reduce.2.cloned.1.call-update) | async-done | bytes 524304 | tf_op jit(solution)/shard_map/psum | solution.py:61
  351.8 1.3 constant_dynamic-slice_fusion
  (14 shorter events, 0.2 us)
Async XLA Ops:
  6.5 29.3 %all-gather.3.cloned.1.call-start = ((), (), s32[]{:S(2)}) async-start(), calls=%async_computation.1 | async-start | bytes 1572864 | tf_op jit(solution)/shard_map/all_gather | solution.py:14
  7.3 86.4 %all-gather.5.cloned.1.call-start = ((), (), s32[]{:S(2)}) async-start(), calls=%async_computation.2 | async-start | bytes 5242880 | tf_op jit(solution)/shard_map/all_gather | solution.py:14
  39.4 5.4 %copy-start.1 = (s32[2]{0:T(128)S(1)}, s32[2]{0:T(128)}, u32[]{:S(2)}) copy-start(s32[2]{0:T(128)} %param.8) | copy-start | bytes 28
  39.4 54.2 %copy-start.2 = (f32[16]{0:T(128)S(1)}, f32[16]{0:T(128)}, u32[]{:S(2)}) copy-start(f32[16]{0:T(128)} %param.9) | copy-start | bytes 196
  39.4 54.2 %all-to-all-start = ((bf16[8,1,256,1024]{3,2,1,0:T(8,128)(2,1)}), bf16[8,1,256,1024]{3,2,1,0:T(8,128)(2,1)}, u32[]{:S(2)}, u32[]{:S(2)}) async-start(bf16[8,1,256,1024]{3,2,1,0:T(8,128)(2,1)} %stack.44), calls=%async_computation | async-start | bytes 8388608 | tf_op jit(solution)/shard_map/all_to_all | solution.py:53
  44.8 306.9 %all-reduce.2.cloned.1.call-start = ((), (), s32[]{:S(2)}) async-start(), calls=%async_computation.3 | async-start | bytes 1048576 | tf_op jit(solution)/shard_map/psum | solution.py:61
  204.9 0.8 copy-start
Sparse Core Ops, SparseCore 0:
  9.0 26.8 all-gather.2
  37.5 49.1 all-gather.4
  205.8 145.8 all-reduce.1
